TPU v7x, 256 devices: a whole 4x4x8 slice. The times are simulated.
256 devices in a mesh: slab: 64 (over x, z, core), img: 4 (over y).
Axes of the slice: x: 4, y: 4, z: 8, core: 2. Of those that a mesh axis runs over, the one named last changes fastest.
Arguments:
- volume: bfloat16 [32768, 256], P('slab'), may hold values from -6 to 6
- interp: bfloat16 [4, 64, 16, 32768], P('img', None, None, 'slab'), may hold values from -0.09375 to 0.09375
- block_index: int32 [4, 64, 64], P('img'), may hold values from 0 to 7
- images: bfloat16 [4, 1024, 128, 256], P('img', 'slab'), may hold values from -6 to 6
- defocus: float32 [4, 1024], P('img', 'slab'), may hold values from 5000 to 25000
- orient: int32 [4, 1024, 4], P('img', 'slab'), may hold values from 0 to 63, all different within a row
Outputs:
- update: float32 [32768, 256], P('slab')
- weights: float32 [4, 1024, 64], P('img', 'slab')
Inputs may be any that keep to these rules, and one draw needn't show every extreme that they name: `orient`: each image lists 4 different orientations of its group.
All inputs are finite; a program needn't handle non-finite values.
Results may differ from a plain program's by a relative error of at most 0.0077.
Values may be sent and summed in bfloat16 or wider, within the bound.
A program may use at most 64 MiB of HBM per device.

v0:
```python
import math
import jax
import jax.numpy as jnp
from jax import lax
from jax.sharding import PartitionSpec as P

BOX = 256
NS = 16
wave_length = 0.0197
aberration = 27000000.0
amplitude = 0.1
grid_side = 4


def phase_tables(fourier, shifts, box):
    freq = (jnp.arange(fourier, dtype=jnp.int32) - fourier // 2).astype(jnp.float32)
    shift_steps = jnp.arange(shifts, dtype=jnp.int32)
    shift_x = (2 * (shift_steps // grid_side) - (grid_side - 1)).astype(jnp.float32)
    shift_y = (2 * (shift_steps % grid_side) - (grid_side - 1)).astype(jnp.float32)
    angle = 2.0 * math.pi / box * (freq[:, None, None] * shift_x + freq[None, :, None] * shift_y)
    forward = jnp.stack([jnp.cos(angle), jnp.sin(angle)], axis=1).reshape(
        2 * fourier * fourier, shifts
    )
    backward = jnp.stack([jnp.cos(angle), -jnp.sin(angle)], axis=1).reshape(
        2 * fourier * fourier, shifts
    )
    return (forward.astype(jnp.bfloat16), backward.T.astype(jnp.bfloat16))


def contrast(defocus_blk, fourier, box):
    freq = (jnp.arange(fourier, dtype=jnp.int32) - fourier // 2).astype(jnp.float32)
    wave_sq = (freq[:, None] * freq[:, None] + freq[None, :] * freq[None, :]) / (box * box)
    phase = math.pi * wave_length * defocus_blk[:, None, None] * wave_sq
    phase = phase - 0.5 * math.pi * aberration * wave_length**3 * wave_sq * wave_sq
    return -(math.sqrt(1.0 - amplitude * amplitude) * jnp.sin(phase) + amplitude * jnp.cos(phase))


def correlate(panels, image_blk, list_blk, defocus_blk, phase_fwd, phase_back, box):
    count = image_blk.shape[0]
    fourier = image_blk.shape[1]
    picks = list_blk.shape[1]
    shifts = phase_fwd.shape[1]
    ctf = contrast(defocus_blk, fourier, box)
    weighted = ctf[:, :, None, :] * image_blk.astype(jnp.float32).reshape(
        count, fourier, 2, fourier
    )
    real_u = weighted[:, None, :, 0]
    imag_u = weighted[:, None, :, 1]
    chosen = panels[list_blk].astype(jnp.float32).reshape(count, picks, fourier, 2, fourier)
    real_p = chosen[:, :, :, 0]
    imag_p = chosen[:, :, :, 1]
    product = jnp.stack(
        [real_p * real_u + imag_p * imag_u, real_p * imag_u - imag_p * real_u], axis=3
    )
    product = product.astype(jnp.bfloat16).reshape(count * picks, 2 * fourier * fourier)
    scores = jnp.dot(product, phase_fwd, preferred_element_type=jnp.float32) / fourier
    scores = scores.reshape(count, picks * shifts)
    squared = scores * scores
    weights = squared / (jnp.mean(squared, axis=1, keepdims=True) + 1e-05)
    rounded = weights.astype(jnp.bfloat16).reshape(count * picks, shifts)
    spread = jnp.dot(rounded, phase_back, preferred_element_type=jnp.float32)
    spread = spread.reshape(count, picks, fourier, 2, fourier)
    real_e = spread[:, :, :, 0]
    imag_e = spread[:, :, :, 1]
    backed = jnp.stack(
        [real_u * real_e - imag_u * imag_e, real_u * imag_e + imag_u * real_e], axis=3
    )
    backed = backed.astype(jnp.bfloat16).reshape(count * picks, 2 * fourier * fourier)
    return (weights, backed)


def on_device(volume, interp, block_index, images, defocus, orient):
    slab_count = lax.axis_size("slab")
    slab_index = lax.axis_index("slab")
    orient_count = interp.shape[1]
    ori_dev = orient_count // slab_count
    block_rows = interp.shape[2]
    fourier = images.shape[2]
    block_count = fourier // block_rows
    img_dev = images.shape[1]
    picks = orient.shape[2]
    levels = jnp.arange(block_count, dtype=jnp.int32)
    partial_value = jnp.einsum("jpr,rx->jpx", interp[0], volume, preferred_element_type=jnp.float32)
    owned_idx = lax.dynamic_slice_in_dim(block_index[0], slab_index * ori_dev, ori_dev, 0)
    received = lax.all_to_all(
        partial_value.reshape(slab_count, ori_dev * block_rows, 2 * fourier),
        "slab",
        split_axis=0,
        concat_axis=0,
        tiled=True,
    ).reshape(slab_count, ori_dev, block_rows, 2 * fourier)
    place = (owned_idx[:, :, None] == levels).astype(jnp.float32)
    summed = jnp.einsum(
        "osb,sopx->obpx",
        place,
        received,
        precision=lax.Precision.HIGHEST,
        preferred_element_type=jnp.float32,
    ).reshape(ori_dev, fourier, 2 * fourier)
    panels = lax.all_gather(summed.astype(jnp.bfloat16), "slab", axis=0, tiled=True)
    phase_fwd, phase_back = phase_tables(fourier, NS, BOX)
    blk = math.gcd(img_dev, 32)
    blk_total = img_dev // blk

    def per_block(pieces):
        image_blk, list_blk, defocus_blk = pieces
        return correlate(panels, image_blk, list_blk, defocus_blk, phase_fwd, phase_back, BOX)

    weights, backs = lax.map(
        per_block,
        (
            images[0].reshape(blk_total, blk, fourier, 2 * fourier),
            orient[0].reshape(blk_total, blk, picks),
            defocus[0].reshape(blk_total, blk),
        ),
    )
    all_slices = backs.reshape(img_dev * picks, 2 * fourier * fourier)
    member = (
        orient[0].reshape(-1)[:, None] == jnp.arange(orient_count, dtype=jnp.int32)[None, :]
    ).astype(jnp.bfloat16)
    contrib = lax.dot_general(
        member, all_slices, (((0,), (0,)), ((), ())), preferred_element_type=jnp.float32
    ).reshape(orient_count, fourier, 2 * fourier)
    gathered = lax.all_to_all(
        contrib.astype(jnp.bfloat16), "slab", split_axis=0, concat_axis=0, tiled=True
    ).reshape(slab_count, ori_dev, fourier, 2 * fourier)
    back_own = jnp.sum(gathered.astype(jnp.float32), axis=0).astype(jnp.bfloat16)
    back_own = back_own.reshape(ori_dev, block_count, block_rows, 2 * fourier)
    chosen_back = (owned_idx[:, :, None] == levels).astype(jnp.bfloat16)
    outgoing = jnp.einsum(
        "osb,obpx->sopx", chosen_back, back_own, preferred_element_type=jnp.float32
    )
    outgoing = outgoing.astype(jnp.bfloat16).reshape(slab_count * ori_dev, block_rows, 2 * fourier)
    incoming = lax.all_to_all(outgoing, "slab", split_axis=0, concat_axis=0, tiled=True)
    column = jnp.einsum("jpr,jpx->rx", interp[0], incoming, preferred_element_type=jnp.float32)
    summed_cols = lax.psum(column, "img")
    update = summed_cols / math.sqrt(img_dev * slab_count)
    return (update, weights)


def solution(mesh):
    return jax.shard_map(
        on_device,
        mesh=mesh,
        in_specs=(
            P("slab", None),
            P("img", None, None, "slab"),
            P("img", None, None),
            P("img", "slab", None, None),
            P("img", "slab"),
            P("img", "slab", None),
        ),
        out_specs=(P("slab", None), P("img", "slab", None)),
        check_vma=False,
    )
```

profile of v0, /device:TPU:2, one launch (start us, length us, event | category | flops | bytes accessed | tf_op | source)
XLA Modules:
  0.0 393.0 jit_solution(16889548143787505688)
XLA Ops:
  7.2 1.2 copy-done
  8.4 2.4 fusion.13
  10.8 12.0 %all-to-all-start = ((f32[64,16,256]{2,1,0:T(8,128)}), f32[64,16,256]{2,1,0:T(8,128)S(1)}, u32[]{:S(2)}, u32[]{:S(2)}) async-start(f32[64,16,256]{2,1,0:T(8,128)} %fusion.13), calls=%async_computation | async-start | bytes 2097152 | tf_op jit(solution)/shard_map/all_to_all | solution.py:85
  22.8 0.7 dynamic-slice_bitcast_fusion
  23.5 26.4 %all-to-all-done = f32[64,16,256]{2,1,0:T(8,128)S(1)} async-done(((f32[64,16,256]{2,1,0:T(8,128)}), f32[64,16,256]{2,1,0:T(8,128)S(1)}, u32[]{:S(2)}, u32[]{:S(2)}) %all-to-all-start) | async-done | bytes 1048608 | tf_op jit(solution)/shard_map/all_to_all | solution.py:85
  49.9 1.0 convolution_convert_fusion.1
  50.9 0.6 copy.61
  51.6 0.2 all-reduce.2.cloned.1.call-start
  52.1 2.1 reshape.433
  54.3 0.1 copy.67
  54.4 5.4 %fusion.17 = (bf16[128,1,128,16]{2,3,1,0:T(8,128)(2,1)S(1)}, bf16[128,1,128,16]{2,3,1,0:T(8,128)(2,1)}, bf16[128,1,128,16]{2,3,1,0:T(8,128)(2,1)S(1)}) fusion(f32[128,16]{0,1:T(8,128)S(1)} %get-tuple-element.51, f32[128,16]{1,0:T(8,128)S(1)} %copy.67), kind=kLoop, calls=%fused_computation.33 | loop fusion | flops 1572864 | bytes 1589248 | tf_op jit(solution)/shard_map/convert.8
  59.8 0.8 copy-done.2
  60.7 1.9 copy.68
  62.6 2.6 convert_element_type.150
  65.4 3.9 add_negate_fusion
  69.3 1.2 copy_multiply_fusion
  70.5 1.1 slice_bitcast_fusion.1
  71.7 56.5 %all-gather.2.cloned.1.call-done = bf16[64,128,256]{2,1,0:T(8,128)(2,1)} async-done(((bf16[1,128,256]{2,1,0:T(8,128)(2,1)}), bf16[64,128,256]{2,1,0:T(8,128)(2,1)}) %all-gather.2.cloned.1.call-update) | async-done | bytes 4194320 | tf_op jit(solution)/shard_map/all_gather | solution.py:100
  128.2 5.0 %gather_fusion = bf16[64,128,256]{2,1,0:T(8,128)(2,1)} fusion(bf16[64,128,256]{2,1,0:T(8,128)(2,1)} %all-gather.2.cloned.1.call-done, s32[1024]{0:T(1024)S(1)} %pad_clamp_fusion), kind=kCustom, calls=%fused_computation | custom fusion | bytes 8388864 | tf_op jit(solution)/shard_map/while/body/eval_jaxpr/gather | solution.py:49
  133.1 7.0 %copy.63 = f32[64,128,256]{1,2,0:T(8,128)} copy(bf16[64,128,256]{2,1,0:T(8,128)(2,1)} %gather_fusion) | data formatting | bytes 12582912 | tf_op jit(solution)/shard_map/while/body/eval_jaxpr/convert_element_type | solution.py:49
  140.1 7.8 %fusion.39 = (f32[16,4,128,1,128]{2,4,3,1,0:T(8,128)}, f32[16,4,128,1,128]{2,4,3,1,0:T(8,128)}) fusion(f32[16,4,128,2,128]{2,4,3,1,0:T(8,128)} %bitcast.64), kind=kLoop, calls=%fused_computation.74 | loop fusion | bytes 16777216 | tf_op jit(solution)/shard_map/while/body/eval_jaxpr/slice | solution.py:50
  147.9 5.5 %copy.83 = f32[16,4,128,1,128]{4,0,3,2,1:T(8,128)} copy(f32[16,4,128,1,128]{2,4,3,1,0:T(8,128)} %get-tuple-element.41) | data formatting | bytes 8388608
  153.4 5.5 %copy.84 = f32[16,4,128,1,128]{4,0,3,2,1:T(8,128)} copy(f32[16,4,128,1,128]{2,4,3,1,0:T(8,128)} %get-tuple-element.42) | data formatting | bytes 8388608
  158.9 4.9 %add_convert_fusion.1 = (bf16[16,4,128,1,128]{4,0,3,2,1:T(8,128)(2,1)S(1)}, bf16[16,4,128,1,128]{4,0,3,2,1:T(8,128)(2,1)S(1)}) fusion(f32[16,4,128,1,128]{4,0,3,2,1:T(8,128)} %copy.84, f32[16,4,128,1,128]{4,0,3,2,1:T(8,128)} %copy.83, f32[16,128,128]{2,0,1:T(8,128)} %get-tuple-element.44, f32[16,128,128]{2,0,1:T(8,128)S(1)} %get-tuple-element.43), kind=kLoop, calls=%fused_computation.9 | loop fusion | flops 8388608 | bytes 14680064 | tf_op jit(solution)/shard_map/convert.9
  163.8 0.4 pad_maximum_fusion
  164.2 6.6 %copy.66 = bf16[16,4,128,2,128]{4,3,2,1,0:T(2,128)(2,1)} copy(bf16[16,4,128,2,128]{4,0,3,2,1:T(8,128)(2,1)S(1)} %pad_maximum_fusion) | data formatting | bytes 8388608 | tf_op jit(solution)/shard_map/while/body/eval_jaxpr/stack | solution.py:52
  170.8 7.8 %convert_element_type.147 = bf16[64,32768]{1,0:T(8,128)(2,1)} reshape(bf16[16,4,128,2,128]{4,3,2,1,0:T(2,128)(2,1)} %copy.66) | data formatting | bytes 8388608 | tf_op jit(solution)/shard_map/while/body/eval_jaxpr/convert_element_type | solution.py:55
  178.6 3.7 fusion.40
  182.4 0.1 reduce_sum.31
  182.6 0.1 div.68
  182.7 0.1 copy.69
  182.8 2.3 fusion.9
  185.2 1.5 subtract_convert_fusion
  186.7 0.4 pad_maximum_fusion.1
  187.1 6.6 %copy.71 = bf16[16,4,128,2,128]{4,3,2,1,0:T(2,128)(2,1)} copy(bf16[16,4,128,2,128]{4,0,3,2,1:T(8,128)(2,1)S(1)} %pad_maximum_fusion.1) | data formatting | bytes 8388608 | tf_op jit(solution)/shard_map/while/body/eval_jaxpr/stack | solution.py:65
  193.7 7.9 %convert_element_type.152 = bf16[64,32768]{1,0:T(8,128)(2,1)} reshape(bf16[16,4,128,2,128]{4,3,2,1,0:T(2,128)(2,1)} %copy.71) | data formatting | bytes 8388608 | tf_op jit(solution)/shard_map/while/body/eval_jaxpr/convert_element_type | solution.py:68
  201.5 3.4 fusion.3
  204.9 2.4 copy.73
  207.4 102.1 %all_to_all.15 = bf16[64,128,256]{2,1,0:T(8,128)(2,1)} all-to-all(bf16[64,128,256]{2,1,0:T(8,128)(2,1)S(1)} %copy.73), channel_id=1, replica_groups=mesh['slab'=64,'img'=4] {'slab'}, dimensions={0} | all-to-all | bytes 8388608 | tf_op jit(solution)/shard_map/all_to_all | solution.py:124
  309.4 2.8 reduce_sum.32
  312.2 0.3 fusion.6
  312.6 0.3 copy.75
  312.9 24.0 %all_to_all.16 = bf16[64,16,256]{2,1,0:T(8,128)(2,1)S(1)} all-to-all(bf16[64,16,256]{2,1,0:T(8,128)(2,1)S(1)} %copy.75), channel_id=1, replica_groups=mesh['slab'=64,'img'=4] {'slab'}, dimensions={0} | all-to-all | bytes 1048576 | tf_op jit(solution)/shard_map/all_to_all | solution.py:134
  336.9 1.2 convolution_bitcast_fusion
  338.3 0.7 broadcast_divide_fusion
  339.0 45.1 %all-reduce.2.cloned.1.call-done = f32[512,256]{0,1:T(8,128)} async-done(((f32[512,256]{0,1:T(8,128)}), f32[512,256]{0,1:T(8,128)}) %all-reduce.2.cloned.1.call-update) | async-done | bytes 524304 | tf_op jit(solution)/shard_map/psum | solution.py:136
  384.1 1.1 broadcast_multiply_fusion
  385.2 1.0 copy.77
  (32 shorter events, 1.0 us)
Async XLA Ops:
  7.2 1.2 copy-start
  7.2 44.7 %copy-start.4 = (s32[1,16,4]{1,2,0:T(4,128)S(1)}, s32[1,16,4]{1,2,0:T(4,128)}, u32[]{:S(2)}) copy-start(s32[1,16,4]{1,2,0:T(4,128)} %param.11) | copy-start | bytes 772
  10.8 39.2 %all-to-all-start = ((f32[64,16,256]{2,1,0:T(8,128)}), f32[64,16,256]{2,1,0:T(8,128)S(1)}, u32[]{:S(2)}, u32[]{:S(2)}) async-start(f32[64,16,256]{2,1,0:T(8,128)} %fusion.13), calls=%async_computation | async-start | bytes 2097152 | tf_op jit(solution)/shard_map/all_to_all | solution.py:85
  22.8 105.4 %all-gather.2.cloned.1.call-start = ((), (), s32[]{:S(2)}) async-start(), calls=%async_computation.3 | async-start | bytes 4259840 | tf_op jit(solution)/shard_map/all_gather | solution.py:100
  51.6 332.5 %all-reduce.2.cloned.1.call-start = ((), (), s32[]{:S(2)}) async-start(), calls=%async_computation.4 | async-start | bytes 1048576 | tf_op jit(solution)/shard_map/psum | solution.py:136
  54.2 11.1 %copy-start.5 = (f32[1,16]{1,0:T(1,128)S(1)}, f32[1,16]{1,0:T(1,128)}, u32[]{:S(2)}) copy-start(f32[1,16]{1,0:T(1,128)} %param.10) | copy-start | bytes 196
  59.8 0.8 copy-start.2
  178.6 4.3 %copy-start.3 = (bf16[128,1,128,16]{2,3,1,0:T(8,128)(2,1)S(1)}, bf16[128,1,128,16]{2,3,1,0:T(8,128)(2,1)}, u32[]{:S(2)}) copy-start(bf16[128,1,128,16]{2,3,1,0:T(8,128)(2,1)} %copy-done.2) | copy-start | bytes 1572868
  182.8 2.4 copy-start.1
Sparse Core Ops, SparseCore 0:
  51.7 76.3 all-gather.1
  338.3 45.7 all-reduce.1
where the time goes:
time: 394 us; the launch traced here: 393 us
  waiting for transfers between devices  128 us (32%)
  blocking collectives  126 us (32%)
  local copies, waits for them, and re-layouts  75.3 us (19%)
  other arithmetic  22.6 us (6%)
  matrix products  14.5 us (4%)
  between operations  14.3 us (4%)
  starting transfers between devices  12.3 us (3%)
    all_to_all x1, blocking collectives, on_device(): lax.all_to_all(contrib.astype(jnp.bfloat16), 'slab', split_axis=0, concat...  102 us
    all_gather x1, waiting for transfers between devices, on_device(): lax.all_gather(summed.astype(jnp.bfloat16), 'slab', axis=0, tiled=True)  56.5 us
    psum x1, waiting for transfers between devices, on_device(): summed_cols = lax.psum(column, 'img')  45.1 us
    all_to_all x1, waiting for transfers between devices, on_device(): lax.all_to_all(partial_value.reshape(slab_count, ori_dev * block_rows, 2...  26.4 us
    all_to_all x1, blocking collectives, on_device(): lax.all_to_all(outgoing, 'slab', split_axis=0, concat_axis=0, tiled=True)  24 us
    unnamed x16, local copies, waits for them, and re-layouts  14.1 us
    all_to_all x1, starting transfers between devices, on_device(): lax.all_to_all(partial_value.reshape(slab_count, ori_dev * block_rows, 2...  12 us
    another operation x3, other arithmetic  11.8 us
  transfers between devices with their start and end apart: 3, of which 3 were waited for; matrix products, arithmetic and copies ran while one was open for 5% of the time, Pallas kernels for 0%

commit v1 on v0

--- a/solution.py
+++ b/solution.py
@@ -97,7 +97,12 @@
         precision=lax.Precision.HIGHEST,
         preferred_element_type=jnp.float32,
     ).reshape(ori_dev, fourier, 2 * fourier)
-    panels = lax.all_gather(summed.astype(jnp.bfloat16), "slab", axis=0, tiled=True)
+    panels = jnp.concatenate(
+        lax.all_to_all(
+            jnp.stack([summed.astype(jnp.bfloat16)] * lax.axis_size("slab")), "slab", 0, 0
+        ),
+        axis=0,
+    )
     phase_fwd, phase_back = phase_tables(fourier, NS, BOX)
     blk = math.gcd(img_dev, 32)
     blk_total = img_dev // blk

time: 394 us -> 422 us (1.071)
  waiting for transfers between devices: 128 us -> 146 us
  starting transfers between devices: 12.3 us -> 20.2 us
    all_to_all x0 -> x1, waiting for transfers between devices: none -> 74.7 us  [on_device(): lax.all_to_all(jnp.stack([summed.astype(jnp.bfloat16)] * lax.axis_size('s...]
    all_gather x1 -> x0, waiting for transfers between devices: 56.5 us -> none  [on_device(): lax.all_gather(summed.astype(jnp.bfloat16), 'slab', axis=0, tiled=True)]
    all_to_all x0 -> x1, starting transfers between devices: none -> 7.94 us  [on_device(): lax.all_to_all(jnp.stack([summed.astype(jnp.bfloat16)] * lax.axis_size('s...]
where the time goes in v1:
time: 422 us; the launch traced here: 420 us
  waiting for transfers between devices  146 us (35%)
  blocking collectives  125 us (30%)
  local copies, waits for them, and re-layouts  77.3 us (18%)
  other arithmetic  22.6 us (5%)
  starting transfers between devices  20.2 us (5%)
  matrix products  14.5 us (3%)
  between operations  14.3 us (3%)
    all_to_all x1, blocking collectives, on_device(): lax.all_to_all(contrib.astype(jnp.bfloat16), 'slab', split_axis=0, concat...  101 us
    all_to_all x1, waiting for transfers between devices, on_device(): lax.all_to_all(jnp.stack([summed.astype(jnp.bfloat16)] * lax.axis_size('s...  74.7 us
    psum x1, waiting for transfers between devices, on_device(): summed_cols = lax.psum(column, 'img')  45.3 us
    all_to_all x1, waiting for transfers between devices, on_device(): lax.all_to_all(partial_value.reshape(slab_count, ori_dev * block_rows, 2...  26.4 us
    all_to_all x1, blocking collectives, on_device(): lax.all_to_all(outgoing, 'slab', split_axis=0, concat_axis=0, tiled=True)  24 us
    unnamed x16, local copies, waits for them, and re-layouts  14.1 us
    all_to_all x1, starting transfers between devices, on_device(): lax.all_to_all(partial_value.reshape(slab_count, ori_dev * block_rows, 2...  12 us
    another operation x3, other arithmetic  11.8 us
  transfers between devices with their start and end apart: 3, of which 3 were waited for; matrix products, arithmetic and copies ran while one was open for 5% of the time, Pallas kernels for 0%

profile of v1, /device:TPU:2, one launch (start us, length us, event | category | flops | bytes accessed | tf_op | source)
XLA Modules:
  0.0 420.4 jit_solution(12538484572159524902)
XLA Ops:
  7.2 1.2 copy-done
  8.4 2.4 fusion.13
  10.8 12.0 %all-to-all-start = ((f32[64,16,256]{2,1,0:T(8,128)}), f32[64,16,256]{2,1,0:T(8,128)S(1)}, u32[]{:S(2)}, u32[]{:S(2)}) async-start(f32[64,16,256]{2,1,0:T(8,128)} %fusion.13), calls=%async_computation | async-start | bytes 2097152 | tf_op jit(solution)/shard_map/all_to_all | solution.py:85
  22.8 0.7 dynamic-slice_bitcast_fusion
  23.5 26.4 %all-to-all-done = f32[64,16,256]{2,1,0:T(8,128)S(1)} async-done(((f32[64,16,256]{2,1,0:T(8,128)}), f32[64,16,256]{2,1,0:T(8,128)S(1)}, u32[]{:S(2)}, u32[]{:S(2)}) %all-to-all-start) | async-done | bytes 1048608 | tf_op jit(solution)/shard_map/all_to_all | solution.py:85
  49.9 1.0 convolution_convert_fusion.1
  51.0 2.5 stack.20
  53.5 7.9 %all-to-all-start.1 = ((bf16[64,1,128,256]{3,2,1,0:T(8,128)(2,1)}), bf16[64,1,128,256]{3,2,1,0:T(8,128)(2,1)}, u32[]{:S(2)}, u32[]{:S(2)}) async-start(bf16[64,1,128,256]{3,2,1,0:T(8,128)(2,1)} %stack.20), calls=%async_computation.1 | async-start | bytes 8388608 | tf_op jit(solution)/shard_map/all_to_all | solution.py:101
  61.4 0.2 all-reduce.2.cloned.1.call-start
  61.9 2.1 reshape.436
  64.1 0.1 copy.62
  64.2 5.4 %fusion.17 = (bf16[128,1,128,16]{2,3,1,0:T(8,128)(2,1)S(1)}, bf16[128,1,128,16]{2,3,1,0:T(8,128)(2,1)}, bf16[128,1,128,16]{2,3,1,0:T(8,128)(2,1)S(1)}) fusion(f32[128,16]{0,1:T(8,128)S(1)} %get-tuple-element.51, f32[128,16]{1,0:T(8,128)S(1)} %copy.62), kind=kLoop, calls=%fused_computation.33 | loop fusion | flops 1572864 | bytes 1589248 | tf_op jit(solution)/shard_map/convert.8
  69.6 0.8 copy-done.2
  70.5 2.0 copy.63
  72.5 2.6 convert_element_type.149
  75.3 3.9 add_negate_fusion
  79.2 1.2 copy_multiply_fusion
  80.4 1.1 slice_bitcast_fusion.1
  81.6 74.7 %all-to-all-done.1 = bf16[64,1,128,256]{3,2,1,0:T(8,128)(2,1)} async-done(((bf16[64,1,128,256]{3,2,1,0:T(8,128)(2,1)}), bf16[64,1,128,256]{3,2,1,0:T(8,128)(2,1)}, u32[]{:S(2)}, u32[]{:S(2)}) %all-to-all-start.1) | async-done | bytes 4194336 | tf_op jit(solution)/shard_map/all_to_all | solution.py:101
  156.3 5.0 %gather_fusion = bf16[64,128,256]{2,1,0:T(8,128)(2,1)} fusion(bf16[64,128,256]{2,1,0:T(8,128)(2,1)} %bitcast.8, s32[1024]{0:T(1024)S(1)} %pad_clamp_fusion), kind=kCustom, calls=%fused_computation | custom fusion | bytes 8388864 | tf_op jit(solution)/shard_map/while/body/eval_jaxpr/gather | solution.py:49
  161.2 7.0 %copy.58 = f32[64,128,256]{1,2,0:T(8,128)} copy(bf16[64,128,256]{2,1,0:T(8,128)(2,1)} %gather_fusion) | data formatting | bytes 12582912 | tf_op jit(solution)/shard_map/while/body/eval_jaxpr/convert_element_type | solution.py:49
  168.2 7.8 %fusion.39 = (f32[16,4,128,1,128]{2,4,3,1,0:T(8,128)}, f32[16,4,128,1,128]{2,4,3,1,0:T(8,128)}) fusion(f32[16,4,128,2,128]{2,4,3,1,0:T(8,128)} %bitcast.65), kind=kLoop, calls=%fused_computation.74 | loop fusion | bytes 16777216 | tf_op jit(solution)/shard_map/while/body/eval_jaxpr/slice | solution.py:50
  176.0 5.5 %copy.82 = f32[16,4,128,1,128]{4,0,3,2,1:T(8,128)} copy(f32[16,4,128,1,128]{2,4,3,1,0:T(8,128)} %get-tuple-element.41) | data formatting | bytes 8388608
  181.5 5.5 %copy.83 = f32[16,4,128,1,128]{4,0,3,2,1:T(8,128)} copy(f32[16,4,128,1,128]{2,4,3,1,0:T(8,128)} %get-tuple-element.42) | data formatting | bytes 8388608
  187.0 4.9 %add_convert_fusion.1 = (bf16[16,4,128,1,128]{4,0,3,2,1:T(8,128)(2,1)S(1)}, bf16[16,4,128,1,128]{4,0,3,2,1:T(8,128)(2,1)S(1)}) fusion(f32[16,4,128,1,128]{4,0,3,2,1:T(8,128)} %copy.83, f32[16,4,128,1,128]{4,0,3,2,1:T(8,128)} %copy.82, f32[16,128,128]{2,0,1:T(8,128)} %get-tuple-element.44, f32[16,128,128]{2,0,1:T(8,128)S(1)} %get-tuple-element.43), kind=kLoop, calls=%fused_computation.9 | loop fusion | flops 8388608 | bytes 14680064 | tf_op jit(solution)/shard_map/convert.9
  191.9 0.4 pad_maximum_fusion
  192.3 6.6 %copy.61 = bf16[16,4,128,2,128]{4,3,2,1,0:T(2,128)(2,1)} copy(bf16[16,4,128,2,128]{4,0,3,2,1:T(8,128)(2,1)S(1)} %pad_maximum_fusion) | data formatting | bytes 8388608 | tf_op jit(solution)/shard_map/while/body/eval_jaxpr/stack | solution.py:52
  198.9 7.8 %convert_element_type.146 = bf16[64,32768]{1,0:T(8,128)(2,1)} reshape(bf16[16,4,128,2,128]{4,3,2,1,0:T(2,128)(2,1)} %copy.61) | data formatting | bytes 8388608 | tf_op jit(solution)/shard_map/while/body/eval_jaxpr/convert_element_type | solution.py:55
  206.7 3.7 fusion.40
  210.5 0.1 reduce_sum.31
  210.8 0.1 copy.64
  210.9 2.4 fusion.9
  213.3 1.5 subtract_convert_fusion
  214.8 0.4 pad_maximum_fusion.1
  215.2 6.6 %copy.66 = bf16[16,4,128,2,128]{4,3,2,1,0:T(2,128)(2,1)} copy(bf16[16,4,128,2,128]{4,0,3,2,1:T(8,128)(2,1)S(1)} %pad_maximum_fusion.1) | data formatting | bytes 8388608 | tf_op jit(solution)/shard_map/while/body/eval_jaxpr/stack | solution.py:65
  221.8 7.9 %convert_element_type.151 = bf16[64,32768]{1,0:T(8,128)(2,1)} reshape(bf16[16,4,128,2,128]{4,3,2,1,0:T(2,128)(2,1)} %copy.66) | data formatting | bytes 8388608 | tf_op jit(solution)/shard_map/while/body/eval_jaxpr/convert_element_type | solution.py:68
  229.6 3.4 fusion.3
  233.1 2.4 copy.68
  235.5 101.2 %all_to_all.20 = bf16[64,128,256]{2,1,0:T(8,128)(2,1)} all-to-all(bf16[64,128,256]{2,1,0:T(8,128)(2,1)S(1)} %copy.68), channel_id=1, replica_groups=mesh['slab'=64,'img'=4] {'slab'}, dimensions={0} | all-to-all | bytes 8388608 | tf_op jit(solution)/shard_map/all_to_all | solution.py:129
  336.6 2.8 reduce_sum.32
  339.4 0.3 fusion.6
  339.8 0.3 copy.70
  340.1 24.0 %all_to_all.21 = bf16[64,16,256]{2,1,0:T(8,128)(2,1)S(1)} all-to-all(bf16[64,16,256]{2,1,0:T(8,128)(2,1)S(1)} %copy.70), channel_id=1, replica_groups=mesh['slab'=64,'img'=4] {'slab'}, dimensions={0} | all-to-all | bytes 1048576 | tf_op jit(solution)/shard_map/all_to_all | solution.py:139
  364.1 1.2 convolution_bitcast_fusion
  365.5 0.7 broadcast_divide_fusion
  366.2 45.3 %all-reduce.2.cloned.1.call-done = f32[512,256]{0,1:T(8,128)} async-done(((f32[512,256]{0,1:T(8,128)}), f32[512,256]{0,1:T(8,128)}) %all-reduce.2.cloned.1.call-update) | async-done | bytes 524304 | tf_op jit(solution)/shard_map/psum | solution.py:141
  411.5 1.1 broadcast_multiply_fusion
  412.6 1.0 copy.74
  (32 shorter events, 1.1 us)
Async XLA Ops:
  7.2 1.2 copy-start
  10.8 39.2 %all-to-all-start = ((f32[64,16,256]{2,1,0:T(8,128)}), f32[64,16,256]{2,1,0:T(8,128)S(1)}, u32[]{:S(2)}, u32[]{:S(2)}) async-start(f32[64,16,256]{2,1,0:T(8,128)} %fusion.13), calls=%async_computation | async-start | bytes 2097152 | tf_op jit(solution)/shard_map/all_to_all | solution.py:85
  53.5 8.2 %copy-start.4 = (s32[1,16,4]{1,2,0:T(4,128)S(1)}, s32[1,16,4]{1,2,0:T(4,128)}, u32[]{:S(2)}) copy-start(s32[1,16,4]{1,2,0:T(4,128)} %param.11) | copy-start | bytes 772
  53.5 102.8 %all-to-all-start.1 = ((bf16[64,1,128,256]{3,2,1,0:T(8,128)(2,1)}), bf16[64,1,128,256]{3,2,1,0:T(8,128)(2,1)}, u32[]{:S(2)}, u32[]{:S(2)}) async-start(bf16[64,1,128,256]{3,2,1,0:T(8,128)(2,1)} %stack.20), calls=%async_computation.1 | async-start | bytes 8388608 | tf_op jit(solution)/shard_map/all_to_all | solution.py:101
  61.4 350.1 %all-reduce.2.cloned.1.call-start = ((), (), s32[]{:S(2)}) async-start(), calls=%async_computation.4 | async-start | bytes 1048576 | tf_op jit(solution)/shard_map/psum | solution.py:141
  64.0 11.2 %copy-start.5 = (f32[1,16]{1,0:T(1,128)S(1)}, f32[1,16]{1,0:T(1,128)}, u32[]{:S(2)}) copy-start(f32[1,16]{1,0:T(1,128)} %param.10) | copy-start | bytes 196
  69.6 0.8 copy-start.2
  206.7 4.3 %copy-start.3 = (bf16[128,1,128,16]{2,3,1,0:T(8,128)(2,1)S(1)}, bf16[128,1,128,16]{2,3,1,0:T(8,128)(2,1)}, u32[]{:S(2)}) copy-start(bf16[128,1,128,16]{2,3,1,0:T(8,128)(2,1)} %copy-done.2) | copy-start | bytes 1572868
  210.9 2.4 copy-start.1
Sparse Core Ops, SparseCore 0:
  365.5 45.9 all-reduce.1
